TPU v7x, 256 devices: a whole 4x4x8 slice. The times are simulated.
256 devices in a mesh: seq: 32 (over x_hi, z, core), batch: 8 (over x_lo, y).
Axes of the slice: x: 4 (x_hi: 2, x_lo: 2; x = x_hi * 2 + x_lo), y: 4, z: 8, core: 2. Of those that a mesh axis runs over, the one named last changes fastest.
Arguments:
- bases: int32 [65536, 128], P(('batch', 'seq')), parts along dimension 0, may hold values from 0 to 3
- embed_table: bfloat16 [512, 768], replicated, may hold values from -0.5 to 0.5
- norm_gains: float32 [3, 768], replicated, may hold values from 0.1 to 1.9
- depth_taps: float32 [3, 5, 768], replicated, may hold values from -2.5 to 2.5
- point_weight: bfloat16 [3, 768, 768], replicated, may hold values from -0.21875 to 0.21875
- query_weight: bfloat16 [768, 128], replicated, may hold values from -0.5390625 to 0.5390625
- key_weight: bfloat16 [768, 128], replicated, may hold values from -0.5390625 to 0.5390625
- pair_kernel: bfloat16 [3, 3, 128, 128], replicated, may hold values from -0.1875 to 0.1875
Outputs:
- trunk: bfloat16 [65536, 768], P(('batch', 'seq')), parts along dimension 0
- pair_map: bfloat16 [4096, 512, 128], P(('batch', 'seq')), parts along dimension 0
There are 8 independent parts, one for each index of `batch`. A program takes and returns all parts, laid end to end along the dimension named above; an argument that names none is the same for every part. Nothing has to cross between parts.
All inputs are finite; a program needn't handle non-finite values.
Results may differ from a plain program's by a relative error of at most 0.018.
Values may be sent and summed in bfloat16 or wider, within the bound.
No kernel may reach another device: no remote copies, remote signals or barrier semaphores. Data moves between devices by JAX's collectives and lax.ppermute only.
A program may use at most 64 MiB of HBM per device.

v0:
```python
import jax
import jax.numpy as jnp
from jax import lax
from jax.sharding import PartitionSpec as P

KW = 5
FIRST_DILATION = 2
SECOND_DILATION = 8
THIRD_DILATION = 32
POOL = 16


def with_halo(cells, sides, width):
    for axis, dim in sides:
        count = lax.axis_size(axis)
        ends = count - 1
        head = lax.slice_in_dim(cells, 0, width, axis=dim)
        tail = lax.slice_in_dim(cells, cells.shape[dim] - width, cells.shape[dim], axis=dim)
        cells = jnp.concatenate(
            [
                lax.ppermute(tail, axis, [(i, (i + 1) % count) for i in range(ends)]),
                cells,
                lax.ppermute(head, axis, [((i + 1) % count, i) for i in range(ends)]),
            ],
            axis=dim,
        )
    return cells


def embed_bases(bases, embed_table):
    one_hot_bases = (bases[:, :, None] == jnp.arange(4, dtype=jnp.int32)).astype(jnp.bfloat16)
    one_hot_bases = one_hot_bases.reshape(bases.shape[0], -1)
    return jnp.dot(one_hot_bases, embed_table, preferred_element_type=jnp.float32).astype(
        jnp.bfloat16
    )


def normalize(value_rows, gain):
    floats = value_rows.astype(jnp.float32)
    scale = lax.rsqrt(jnp.mean(floats * floats, axis=-1, keepdims=True) + 1e-06)
    return (floats * scale * gain).astype(jnp.bfloat16)


def mix_rows(inner, normed, taps, point, dilation_reach, rows):
    summed = jnp.zeros((rows, normed.shape[1]), jnp.float32)
    for offset in range(KW):
        summed = (
            summed
            + normed[offset * dilation_reach : offset * dilation_reach + rows].astype(jnp.float32)
            * taps[offset]
        )
    activated = jax.nn.gelu(summed).astype(jnp.bfloat16)
    return (
        inner.astype(jnp.float32) + jnp.dot(activated, point, preferred_element_type=jnp.float32)
    ).astype(jnp.bfloat16)


def pair_conv(extended, pair_kernel, rows, width):
    padded = jnp.pad(extended, ((0, 0), (1, 1), (0, 0)))
    channels = extended.shape[2]
    summed = jnp.zeros((rows * width, channels), jnp.float32)
    for row_tap in range(3):
        for col_tap in range(3):
            window = padded[row_tap : row_tap + rows, col_tap : col_tap + width].reshape(
                rows * width, channels
            )
            summed = summed + jnp.dot(
                window, pair_kernel[row_tap, col_tap], preferred_element_type=jnp.float32
            )
    center = extended[1 : rows + 1].astype(jnp.float32).reshape(rows * width, channels)
    return (center + jax.nn.gelu(summed)).astype(jnp.bfloat16).reshape(rows, width, channels)


def on_device(
    bases, embed_table, norm_gains, depth_taps, point_weight, query_weight, key_weight, pair_kernel
):
    dilation_reaches = (FIRST_DILATION, SECOND_DILATION, THIRD_DILATION)
    current = embed_bases(bases, embed_table)
    slab_rows = current.shape[0]
    for trunk_layer in range(3):
        dilation_reach = dilation_reaches[trunk_layer]
        normed = normalize(current, norm_gains[trunk_layer])
        widened = with_halo(normed, (("seq", 0),), 2 * dilation_reach)
        current = mix_rows(
            current,
            widened,
            depth_taps[trunk_layer],
            point_weight[trunk_layer],
            dilation_reach,
            slab_rows,
        )
    pooled = jnp.mean(
        current.astype(jnp.float32).reshape(-1, POOL, current.shape[1]), axis=1
    ).astype(jnp.bfloat16)
    queries = jnp.dot(pooled, query_weight, preferred_element_type=jnp.float32).astype(jnp.bfloat16)
    all_keys = jnp.dot(
        lax.all_gather(pooled, "seq", axis=0, tiled=True),
        key_weight,
        preferred_element_type=jnp.float32,
    ).astype(jnp.bfloat16)
    key_floats = all_keys.astype(jnp.float32)[None, :, :]
    pair_rows = queries.shape[0]
    pair = (queries.astype(jnp.float32)[:, None, :] * key_floats).astype(jnp.bfloat16)
    extended = with_halo(pair, (("seq", 0),), 1)
    pair_map = pair_conv(extended, pair_kernel, pair_rows, all_keys.shape[0])
    return (current, pair_map)


def solution(mesh):
    return jax.shard_map(
        on_device,
        mesh=mesh,
        in_specs=(P(("batch", "seq"), None), P(), P(), P(), P(), P(), P(), P()),
        out_specs=(P(("batch", "seq"), None), P(("batch", "seq"), None, None)),
        check_vma=False,
    )
```

profile of v0, /device:TPU:14, one launch (start us, length us, event | category | flops | bytes accessed | tf_op | source)
XLA Modules:
  0.0 109.2 jit_solution(7016129010796559855)
XLA Ops:
  0.6 0.0 copy-start
  0.6 0.8 slice_reduce_fusion.5
  1.5 0.1 eq.23
  1.6 1.0 copy.10
  2.6 0.0 copy-start.5
  2.6 0.1 eq.20
  2.7 0.2 eq.21
  2.9 0.0 copy-done
  2.9 0.7 multiply_reduce_fusion.2
  3.6 0.1 multiply_convert_fusion.3
  3.8 1.9 %collective-permute-start = (bf16[4,768]{1,0:T(4,128)(2,1)S(1)}, bf16[4,768]{1,0:T(4,128)(2,1)S(1)}, u32[]{:S(2)}, u32[]{:S(2)}) collective-permute-start(bf16[4,768]{1,0:T(4,128)(2,1)S(1)} %get-tuple-element.34), channel_id=1, source_target_pairs={{0,8},{8,16},{16,24},{24,32},{32,40},{40,48},{48,56},{56,64},{64,7... | collective-permute-start | bytes 18440 | tf_op jit(solution)/shard_map/ppermute | solution.py:21
  5.7 8.0 %collective-permute-start.1 = (bf16[4,768]{1,0:T(4,128)(2,1)S(1)}, bf16[4,768]{1,0:T(4,128)(2,1)S(1)}, u32[]{:S(2)}, u32[]{:S(2)}) collective-permute-start(bf16[4,768]{1,0:T(4,128)(2,1)S(1)} %get-tuple-element.35), channel_id=1, source_target_pairs={{8,0},{16,8},{24,16},{32,24},{40,32},{48,40},{56,48},{64,56},{72,6... | collective-permute-start | bytes 18440 | tf_op jit(solution)/shard_map/ppermute | solution.py:23
  13.8 0.0 copy-done.5
  13.8 0.1 slice_reduce_fusion.4
  13.9 0.0 collective-permute-done
  13.9 1.2 %collective-permute-done.1 = bf16[4,768]{1,0:T(4,128)(2,1)S(1)} collective-permute-done((bf16[4,768]{1,0:T(4,128)(2,1)S(1)}, bf16[4,768]{1,0:T(4,128)(2,1)S(1)}, u32[]{:S(2)}, u32[]{:S(2)}) %collective-permute-start.1) | collective-permute-done | bytes 6176 | tf_op jit(solution)/shard_map/ppermute | solution.py:23
  15.1 0.0 copy-start.6
  15.1 2.6 %multiply_reduce_fusion.1 = (f32[256]{0:T(256)S(1)}, f32[256,768]{1,0:T(8,128)S(1)}) fusion(f32[256,768]{1,0:T(8,128)S(1)} %get-tuple-element.37, bf16[3,768,768]{2,1,0:T(8,128)(2,1)} %param.12, bf16[256,768]{1,0:T(8,128)(2,1)S(1)} %multiply_convert_fusion.3, bf16[4,768]{1,0:T(4,128)(2,1)S(1)} %collective-permute-done.1, ...), kind=kOutput, calls=%fused_computation.80 | convolution fusion | flops 309853952 | bytes 3174400 | tf_op jit(solution)/shard_map/dot_general | solution.py:54
  17.7 0.1 multiply_convert_fusion.2
  17.9 1.9 %collective-permute-start.2 = (bf16[16,768]{1,0:T(8,128)(2,1)S(1)}, bf16[16,768]{1,0:T(8,128)(2,1)S(1)}, u32[]{:S(2)}, u32[]{:S(2)}) collective-permute-start(bf16[16,768]{1,0:T(8,128)(2,1)S(1)} %get-tuple-element.32), channel_id=1, source_target_pairs={{0,8},{8,16},{16,24},{24,32},{32,40},{40,48},{48,56},{56,64},{64,7... | collective-permute-start | bytes 73736 | tf_op jit(solution)/shard_map/ppermute | solution.py:21
  19.8 7.3 %collective-permute-start.3 = (bf16[16,768]{1,0:T(8,128)(2,1)S(1)}, bf16[16,768]{1,0:T(8,128)(2,1)S(1)}, u32[]{:S(2)}, u32[]{:S(2)}) collective-permute-start(bf16[16,768]{1,0:T(8,128)(2,1)S(1)} %get-tuple-element.33), channel_id=1, source_target_pairs={{8,0},{16,8},{24,16},{32,24},{40,32},{48,40},{56,48},{64,56},{72,6... | collective-permute-start | bytes 73736 | tf_op jit(solution)/shard_map/ppermute | solution.py:23
  27.0 0.0 collective-permute-done.2
  27.1 1.5 %collective-permute-done.3 = bf16[16,768]{1,0:T(8,128)(2,1)S(1)} collective-permute-done((bf16[16,768]{1,0:T(8,128)(2,1)S(1)}, bf16[16,768]{1,0:T(8,128)(2,1)S(1)}, u32[]{:S(2)}, u32[]{:S(2)}) %collective-permute-start.3) | collective-permute-done | bytes 24608 | tf_op jit(solution)/shard_map/ppermute | solution.py:23
  28.5 0.0 copy-done.6
  28.6 1.0 multiply_reduce_fusion
  29.5 0.1 multiply_convert_fusion.1
  29.7 1.9 %collective-permute-start.4 = (bf16[64,768]{1,0:T(8,128)(2,1)S(1)}, bf16[64,768]{1,0:T(8,128)(2,1)S(1)}, u32[]{:S(2)}, u32[]{:S(2)}) collective-permute-start(bf16[64,768]{1,0:T(8,128)(2,1)S(1)} %get-tuple-element.30), channel_id=1, source_target_pairs={{0,8},{8,16},{16,24},{24,32},{32,40},{40,48},{48,56},{56,64},{64,7... | collective-permute-start | bytes 294920 | tf_op jit(solution)/shard_map/ppermute | solution.py:21
  31.6 7.3 %collective-permute-start.5 = (bf16[64,768]{1,0:T(8,128)(2,1)S(1)}, bf16[64,768]{1,0:T(8,128)(2,1)S(1)}, u32[]{:S(2)}, u32[]{:S(2)}) collective-permute-start(bf16[64,768]{1,0:T(8,128)(2,1)S(1)} %get-tuple-element.31), channel_id=1, source_target_pairs={{8,0},{16,8},{24,16},{32,24},{40,32},{48,40},{56,48},{64,56},{72,6... | collective-permute-start | bytes 294920 | tf_op jit(solution)/shard_map/ppermute | solution.py:23
  38.9 0.4 collective-permute-done.4
  39.3 1.8 %collective-permute-done.5 = bf16[64,768]{1,0:T(8,128)(2,1)S(1)} collective-permute-done((bf16[64,768]{1,0:T(8,128)(2,1)S(1)}, bf16[64,768]{1,0:T(8,128)(2,1)S(1)}, u32[]{:S(2)}, u32[]{:S(2)}) %collective-permute-start.5) | collective-permute-done | bytes 98336 | tf_op jit(solution)/shard_map/ppermute | solution.py:23
  41.1 0.0 copy-start.4
  41.1 0.0 copy-start.3
  41.1 1.8 %convert_reduce_fusion = (f32[16,768]{1,0:T(8,128)S(1)}, bf16[256,768]{1,0:T(8,128)(2,1)}) fusion(f32[256,768]{1,0:T(8,128)S(1)} %get-tuple-element.41, bf16[3,768,768]{2,1,0:T(8,128)(2,1)S(1)} %copy-done.6, bf16[256,768]{1,0:T(8,128)(2,1)S(1)} %multiply_convert_fusion.1, bf16[64,768]{1,0:T(8,128)(2,1)S(1)} %collective-permute-done.5, ...), kind=kOutput, calls=%fused_computation.76 | convolution fusion | flops 309645312 | bytes 3018752 | tf_op jit(solution)/shard_map/dot_general | solution.py:54
  42.9 39.0 %all_gather.3 = bf16[512,768]{1,0:T(8,128)(2,1)S(1)} all-gather(bf16[16,768]{1,0:T(8,128)(2,1)S(1)} %multiply_convert_fusion.4), channel_id=1, replica_groups=mesh['seq'=32,'batch'=8] {'seq'}, dimensions={0}, use_global_device_ids=true | all-gather | bytes 811008 | tf_op jit(solution)/shard_map/all_gather | solution.py:97
  81.9 0.0 copy-done.4
  81.9 0.1 fusion.29
  82.0 0.0 copy-done.3
  82.0 0.4 fusion.28
  82.4 0.5 multiply_convert_fusion
  82.9 2.3 %collective-permute-start.6 = (bf16[1,512,128]{2,1,0:T(8,128)(2,1)S(1)}, bf16[1,512,128]{2,1,0:T(8,128)(2,1)S(1)}, u32[]{:S(2)}, u32[]{:S(2)}) collective-permute-start(bf16[1,512,128]{2,1,0:T(8,128)(2,1)S(1)} %get-tuple-element.28), channel_id=1, source_target_pairs={{0,8},{8,16},{16,24},{24,32},{32,40},{40,48},{48,56},{56,64},{64,7... | collective-permute-start | bytes 393224 | tf_op jit(solution)/shard_map/ppermute | solution.py:21
  85.2 7.1 %collective-permute-start.7 = (bf16[1,512,128]{2,1,0:T(8,128)(2,1)S(1)}, bf16[1,512,128]{2,1,0:T(8,128)(2,1)S(1)}, u32[]{:S(2)}, u32[]{:S(2)}) collective-permute-start(bf16[1,512,128]{2,1,0:T(8,128)(2,1)S(1)} %get-tuple-element.29), channel_id=1, source_target_pairs={{8,0},{16,8},{24,16},{32,24},{40,32},{48,40},{56,48},{64,56},{72,6... | collective-permute-start | bytes 393224 | tf_op jit(solution)/shard_map/ppermute | solution.py:23
  92.3 0.5 collective-permute-done.6
  92.8 1.8 %collective-permute-done.7 = bf16[1,512,128]{2,1,0:T(8,128)(2,1)S(1)} collective-permute-done((bf16[1,512,128]{2,1,0:T(8,128)(2,1)S(1)}, bf16[1,512,128]{2,1,0:T(8,128)(2,1)S(1)}, u32[]{:S(2)}, u32[]{:S(2)}) %collective-permute-start.7) | collective-permute-done | bytes 131104 | tf_op jit(solution)/shard_map/ppermute | solution.py:23
  94.6 1.4 %fusion.15 = bf16[18,514,128]{2,1,0:T(8,128)(2,1)S(1)} fusion(bf16[1,512,128]{2,1,0:T(8,128)(2,1)S(1)} %collective-permute-done.7, bf16[16,512,128]{2,1,0:T(8,128)(2,1)S(1)} %multiply_convert_fusion, bf16[1,512,128]{2,1,0:T(8,128)(2,1)S(1)} %collective-permute-done.6), kind=kLoop, calls=%fused_computation.26 | loop fusion | flops 14211072 | bytes 4727808 | tf_op jit(solution)/shard_map/concatenate | solution.py:19
  96.1 0.0 copy-start.2
  96.1 3.8 %fusion.133 = (bf16[16,512,128]{2,1,0:T(8,128)(2,1)S(1)}, bf16[16,512,128]{2,1,0:T(8,128)(2,1)S(1)}, bf16[16,512,128]{2,1,0:T(8,128)(2,1)S(1)}, bf16[16,512,128]...) fusion(bf16[18,514,128]{2,1,0:T(8,128)(2,1)S(1)} %fusion.15), kind=kLoop, calls=%fused_computation.199 | loop fusion | bytes 25165824 | tf_op jit(solution)/shard_map/slice | solution.py:64
  99.9 0.0 copy-done.2
  99.9 0.7 fusion.107
  100.6 0.7 fusion.98
  101.3 0.4 pad_maximum_fusion
  101.6 0.7 convolution_add_fusion.6
  102.3 0.7 convolution_add_fusion.5
  103.0 0.7 convolution_add_fusion.4
  103.7 0.7 convolution_add_fusion.3
  104.4 0.7 convolution_add_fusion.2
  105.1 0.7 convolution_add_fusion.1
  105.8 0.0 copy-start.1
  105.8 3.3 %fusion.10 = bf16[8192,128]{1,0:T(8,128)(2,1)} fusion(f32[8192,128]{1,0:T(8,128)S(1)} %fusion.98, f32[8192,128]{1,0:T(8,128)S(1)} %convolution_add_fusion.1, bf16[8192,128]{1,0:T(8,128)(2,1)S(1)} %bitcast.80, bf16[8192,128]{1,0:T(8,128)(2,1)S(1)} %bitcast.72, bf16[3,3,128,128]{3,2,1,0:T(8,128)(2,1)S(1)} %copy-done.2), kind=kOutput, calls=%fused_computation.20 | convolution fusion | flops 282066944 | bytes 14712832 | tf_op jit(solution)/shard_map/dot_general | solution.py:67
  109.2 0.0 copy-done.1
  (9 shorter events, 0.1 us)
Async XLA Ops:
  0.6 2.3 %copy-start = (bf16[512,768]{1,0:T(8,128)(2,1)S(1)}, bf16[512,768]{1,0:T(8,128)(2,1)}, u32[]{:S(2)}) copy-start(bf16[512,768]{1,0:T(8,128)(2,1)} %param.9) | copy-start | bytes 2359300
  2.6 11.1 %copy-start.5 = (f32[3,5,768]{2,0,1:T(4,128)S(1)}, f32[3,5,768]{2,0,1:T(4,128)}, u32[]{:S(2)}) copy-start(f32[3,5,768]{2,0,1:T(4,128)} %param.11) | copy-start | bytes 138244
  3.8 10.1 %collective-permute-start = (bf16[4,768]{1,0:T(4,128)(2,1)S(1)}, bf16[4,768]{1,0:T(4,128)(2,1)S(1)}, u32[]{:S(2)}, u32[]{:S(2)}) collective-permute-start(bf16[4,768]{1,0:T(4,128)(2,1)S(1)} %get-tuple-element.34), channel_id=1, source_target_pairs={{0,8},{8,16},{16,24},{24,32},{32,40},{40,48},{48,56},{56,64},{64,7... | collective-permute-start | bytes 18440 | tf_op jit(solution)/shard_map/ppermute | solution.py:21
  5.7 9.4 %collective-permute-start.1 = (bf16[4,768]{1,0:T(4,128)(2,1)S(1)}, bf16[4,768]{1,0:T(4,128)(2,1)S(1)}, u32[]{:S(2)}, u32[]{:S(2)}) collective-permute-start(bf16[4,768]{1,0:T(4,128)(2,1)S(1)} %get-tuple-element.35), channel_id=1, source_target_pairs={{8,0},{16,8},{24,16},{32,24},{40,32},{48,40},{56,48},{64,56},{72,6... | collective-permute-start | bytes 18440 | tf_op jit(solution)/shard_map/ppermute | solution.py:23
  15.1 13.4 %copy-start.6 = (bf16[3,768,768]{2,1,0:T(8,128)(2,1)S(1)}, bf16[3,768,768]{2,1,0:T(8,128)(2,1)}, u32[]{:S(2)}) copy-start(bf16[3,768,768]{2,1,0:T(8,128)(2,1)} %param.12) | copy-start | bytes 10616836
  17.9 9.2 %collective-permute-start.2 = (bf16[16,768]{1,0:T(8,128)(2,1)S(1)}, bf16[16,768]{1,0:T(8,128)(2,1)S(1)}, u32[]{:S(2)}, u32[]{:S(2)}) collective-permute-start(bf16[16,768]{1,0:T(8,128)(2,1)S(1)} %get-tuple-element.32), channel_id=1, source_target_pairs={{0,8},{8,16},{16,24},{24,32},{32,40},{40,48},{48,56},{56,64},{64,7... | collective-permute-start | bytes 73736 | tf_op jit(solution)/shard_map/ppermute | solution.py:21
  19.8 8.8 %collective-permute-start.3 = (bf16[16,768]{1,0:T(8,128)(2,1)S(1)}, bf16[16,768]{1,0:T(8,128)(2,1)S(1)}, u32[]{:S(2)}, u32[]{:S(2)}) collective-permute-start(bf16[16,768]{1,0:T(8,128)(2,1)S(1)} %get-tuple-element.33), channel_id=1, source_target_pairs={{8,0},{16,8},{24,16},{32,24},{40,32},{48,40},{56,48},{64,56},{72,6... | collective-permute-start | bytes 73736 | tf_op jit(solution)/shard_map/ppermute | solution.py:23
  29.7 9.6 %collective-permute-start.4 = (bf16[64,768]{1,0:T(8,128)(2,1)S(1)}, bf16[64,768]{1,0:T(8,128)(2,1)S(1)}, u32[]{:S(2)}, u32[]{:S(2)}) collective-permute-start(bf16[64,768]{1,0:T(8,128)(2,1)S(1)} %get-tuple-element.30), channel_id=1, source_target_pairs={{0,8},{8,16},{16,24},{24,32},{32,40},{40,48},{48,56},{56,64},{64,7... | collective-permute-start | bytes 294920 | tf_op jit(solution)/shard_map/ppermute | solution.py:21
  31.6 9.5 %collective-permute-start.5 = (bf16[64,768]{1,0:T(8,128)(2,1)S(1)}, bf16[64,768]{1,0:T(8,128)(2,1)S(1)}, u32[]{:S(2)}, u32[]{:S(2)}) collective-permute-start(bf16[64,768]{1,0:T(8,128)(2,1)S(1)} %get-tuple-element.31), channel_id=1, source_target_pairs={{8,0},{16,8},{24,16},{32,24},{40,32},{48,40},{56,48},{64,56},{72,6... | collective-permute-start | bytes 294920 | tf_op jit(solution)/shard_map/ppermute | solution.py:23
  41.1 40.8 %copy-start.4 = (bf16[768,128]{1,0:T(8,128)(2,1)S(1)}, bf16[768,128]{1,0:T(8,128)(2,1)}, u32[]{:S(2)}) copy-start(bf16[768,128]{1,0:T(8,128)(2,1)} %param.13) | copy-start | bytes 589828
  41.1 40.9 %copy-start.3 = (bf16[768,128]{1,0:T(8,128)(2,1)S(1)}, bf16[768,128]{1,0:T(8,128)(2,1)}, u32[]{:S(2)}) copy-start(bf16[768,128]{1,0:T(8,128)(2,1)} %param.14) | copy-start | bytes 589828
  82.9 9.9 %collective-permute-start.6 = (bf16[1,512,128]{2,1,0:T(8,128)(2,1)S(1)}, bf16[1,512,128]{2,1,0:T(8,128)(2,1)S(1)}, u32[]{:S(2)}, u32[]{:S(2)}) collective-permute-start(bf16[1,512,128]{2,1,0:T(8,128)(2,1)S(1)} %get-tuple-element.28), channel_id=1, source_target_pairs={{0,8},{8,16},{16,24},{24,32},{32,40},{40,48},{48,56},{56,64},{64,7... | collective-permute-start | bytes 393224 | tf_op jit(solution)/shard_map/ppermute | solution.py:21
  85.2 9.4 %collective-permute-start.7 = (bf16[1,512,128]{2,1,0:T(8,128)(2,1)S(1)}, bf16[1,512,128]{2,1,0:T(8,128)(2,1)S(1)}, u32[]{:S(2)}, u32[]{:S(2)}) collective-permute-start(bf16[1,512,128]{2,1,0:T(8,128)(2,1)S(1)} %get-tuple-element.29), channel_id=1, source_target_pairs={{8,0},{16,8},{24,16},{32,24},{40,32},{48,40},{56,48},{64,56},{72,6... | collective-permute-start | bytes 393224 | tf_op jit(solution)/shard_map/ppermute | solution.py:23
  96.1 3.8 %copy-start.2 = (bf16[3,3,128,128]{3,2,1,0:T(8,128)(2,1)S(1)}, bf16[3,3,128,128]{3,2,1,0:T(8,128)(2,1)}, u32[]{:S(2)}) copy-start(bf16[3,3,128,128]{3,2,1,0:T(8,128)(2,1)} %param.15) | copy-start | bytes 884740
  105.8 3.3 %copy-start.1 = (bf16[512,768]{1,0:T(8,128)(2,1)S(1)}, bf16[512,768]{1,0:T(8,128)(2,1)}, u32[]{:S(2)}) copy-start(bf16[512,768]{1,0:T(8,128)(2,1)} %param.9) | copy-start | bytes 2359300
where the time goes:
time: 110 us; the launch traced here: 109 us
  blocking collectives  39 us (35%)
  starting transfers between devices  37.7 us (34%)
  matrix products  15.4 us (14%)
  waiting for transfers between devices  7.18 us (7%)
  local copies, waits for them, and re-layouts  6.22 us (6%)
  other arithmetic  2.74 us (2%)
    all_gather x1, blocking collectives, on_device(): lax.all_gather(pooled, 'seq', axis=0, tiled=True)  39 us
    ppermute x4, starting transfers between devices, with_halo(): lax.ppermute(head, axis, [((i + 1) % count, i) for i in range(ends)])  29.7 us
    dot_general x9, matrix products, pair_conv(): jnp.dot(window, pair_kernel[row_tap, col_tap], preferred_element_type=jnp...  8.85 us
    ppermute x4, starting transfers between devices, with_halo(): lax.ppermute(tail, axis, [(i, (i + 1) % count) for i in range(ends)])  8.02 us
    ppermute x4, waiting for transfers between devices, with_halo(): lax.ppermute(head, axis, [((i + 1) % count, i) for i in range(ends)])  6.28 us
    dot_general x3, matrix products, mix_rows(): jnp.dot(activated, point, preferred_element_type=jnp.float32)  5.33 us
    slice x1, local copies, waits for them, and re-layouts, pair_conv(): padded[row_tap:row_tap + rows, col_tap:col_tap + width]  3.77 us
  transfers between devices with their start and end apart: 8, of which 6 were waited for; matrix products, arithmetic and copies ran while one was open for 0% of the time, Pallas kernels for 0%

commit v1 on v0

--- a/solution.py
+++ b/solution.py
@@ -1,3 +1,4 @@
+import functools
 import jax
 import jax.numpy as jnp
 from jax import lax
@@ -8,6 +9,16 @@
 SECOND_DILATION = 8
 THIRD_DILATION = 32
 POOL = 16
+
+
+def forms_put(load, shard_axis):
+    found_now = jnp.stack(lax.axis_size(shard_axis) * [load], 0)
+    x_new = lax.all_to_all(found_now, shard_axis, 0, 0)
+    current_block = jnp.concatenate(x_new, axis=0)
+    return current_block
+
+
+hold_bands_here = functools.partial(forms_put, shard_axis="seq")
 
 
 def with_halo(cells, sides, width):
@@ -94,9 +105,7 @@
     ).astype(jnp.bfloat16)
     queries = jnp.dot(pooled, query_weight, preferred_element_type=jnp.float32).astype(jnp.bfloat16)
     all_keys = jnp.dot(
-        lax.all_gather(pooled, "seq", axis=0, tiled=True),
-        key_weight,
-        preferred_element_type=jnp.float32,
+        hold_bands_here(pooled), key_weight, preferred_element_type=jnp.float32
     ).astype(jnp.bfloat16)
     key_floats = all_keys.astype(jnp.float32)[None, :, :]
     pair_rows = queries.shape[0]

time: 110 us -> 102 us (0.927)
  blocking collectives: 39 us -> 0 us
  waiting for transfers between devices: 7.18 us -> 29.4 us
  starting transfers between devices: 37.7 us -> 45.1 us
    all_gather x1 -> x0, blocking collectives: 39 us -> none  [on_device(): lax.all_gather(pooled, 'seq', axis=0, tiled=True)]
    all_to_all x0 -> x1, waiting for transfers between devices: none -> 22.2 us  [forms_put(): x_new = lax.all_to_all(found_now, shard_axis, 0, 0)]
    all_to_all x0 -> x1, starting transfers between devices: none -> 7.44 us  [forms_put(): x_new = lax.all_to_all(found_now, shard_axis, 0, 0)]
  transfers between devices with their start and end apart: 8 -> 9, of which waited for: 6 -> 7; matrix products, arithmetic and copies ran while one was open for 0% -> 0% of each run, Pallas kernels for 0% -> 0%
where the time goes in v1:
time: 102 us; the launch traced here: 101 us
  starting transfers between devices  45.1 us (44%)
  waiting for transfers between devices  29.4 us (29%)
  matrix products  15.3 us (15%)
  local copies, waits for them, and re-layouts  7.15 us (7%)
  other arithmetic  2.74 us (3%)
    ppermute x4, starting transfers between devices, with_halo(): lax.ppermute(head, axis, [((i + 1) % count, i) for i in range(ends)])  30 us
    all_to_all x1, waiting for transfers between devices, forms_put(): x_new = lax.all_to_all(found_now, shard_axis, 0, 0)  22.2 us
    dot_general x9, matrix products, pair_conv(): jnp.dot(window, pair_kernel[row_tap, col_tap], preferred_element_type=jnp...  8.83 us
    ppermute x4, starting transfers between devices, with_halo(): lax.ppermute(tail, axis, [(i, (i + 1) % count) for i in range(ends)])  7.68 us
    all_to_all x1, starting transfers between devices, forms_put(): x_new = lax.all_to_all(found_now, shard_axis, 0, 0)  7.44 us
    ppermute x4, waiting for transfers between devices, with_halo(): lax.ppermute(head, axis, [((i + 1) % count, i) for i in range(ends)])  6.28 us
    dot_general x3, matrix products, mix_rows(): jnp.dot(activated, point, preferred_element_type=jnp.float32)  5.33 us
    slice x1, local copies, waits for them, and re-layouts, pair_conv(): padded[row_tap:row_tap + rows, col_tap:col_tap + width]  3.77 us
  transfers between devices with their start and end apart: 9, of which 7 were waited for; matrix products, arithmetic and copies ran while one was open for 0% of the time, Pallas kernels for 0%

profile of v1, /device:TPU:14, one launch (start us, length us, event | category | flops | bytes accessed | tf_op | source)
XLA Modules:
  0.0 100.7 jit_solution(4892779338536649351)
XLA Ops:
  0.6 0.0 copy-start
  0.6 0.8 slice_reduce_fusion.5
  1.5 0.1 eq.23
  1.6 1.0 copy.10
  2.6 0.0 copy-start.5
  2.6 0.1 eq.20
  2.7 0.2 eq.21
  2.9 0.0 copy-done
  2.9 0.7 multiply_reduce_fusion.2
  3.6 0.1 multiply_convert_fusion.3
  3.8 1.9 %collective-permute-start = (bf16[4,768]{1,0:T(4,128)(2,1)S(1)}, bf16[4,768]{1,0:T(4,128)(2,1)S(1)}, u32[]{:S(2)}, u32[]{:S(2)}) collective-permute-start(bf16[4,768]{1,0:T(4,128)(2,1)S(1)} %get-tuple-element.34), channel_id=1, source_target_pairs={{0,8},{8,16},{16,24},{24,32},{32,40},{40,48},{48,56},{56,64},{64,7... | collective-permute-start | bytes 18440 | tf_op jit(solution)/shard_map/ppermute | solution.py:32
  5.7 8.0 %collective-permute-start.1 = (bf16[4,768]{1,0:T(4,128)(2,1)S(1)}, bf16[4,768]{1,0:T(4,128)(2,1)S(1)}, u32[]{:S(2)}, u32[]{:S(2)}) collective-permute-start(bf16[4,768]{1,0:T(4,128)(2,1)S(1)} %get-tuple-element.35), channel_id=1, source_target_pairs={{8,0},{16,8},{24,16},{32,24},{40,32},{48,40},{56,48},{64,56},{72,6... | collective-permute-start | bytes 18440 | tf_op jit(solution)/shard_map/ppermute | solution.py:34
  13.8 0.0 copy-done.5
  13.8 0.1 slice_reduce_fusion.4
  13.9 0.0 collective-permute-done
  13.9 1.2 %collective-permute-done.1 = bf16[4,768]{1,0:T(4,128)(2,1)S(1)} collective-permute-done((bf16[4,768]{1,0:T(4,128)(2,1)S(1)}, bf16[4,768]{1,0:T(4,128)(2,1)S(1)}, u32[]{:S(2)}, u32[]{:S(2)}) %collective-permute-start.1) | collective-permute-done | bytes 6176 | tf_op jit(solution)/shard_map/ppermute | solution.py:34
  15.1 0.0 copy-start.6
  15.1 2.6 %multiply_reduce_fusion.1 = (f32[256]{0:T(256)S(1)}, f32[256,768]{1,0:T(8,128)S(1)}) fusion(f32[256,768]{1,0:T(8,128)S(1)} %get-tuple-element.37, bf16[3,768,768]{2,1,0:T(8,128)(2,1)} %param.12, bf16[256,768]{1,0:T(8,128)(2,1)S(1)} %multiply_convert_fusion.3, bf16[4,768]{1,0:T(4,128)(2,1)S(1)} %collective-permute-done.1, ...), kind=kOutput, calls=%fused_computation.80 | convolution fusion | flops 309853952 | bytes 3174400 | tf_op jit(solution)/shard_map/dot_general | solution.py:65
  17.7 0.1 multiply_convert_fusion.2
  17.9 1.9 %collective-permute-start.2 = (bf16[16,768]{1,0:T(8,128)(2,1)S(1)}, bf16[16,768]{1,0:T(8,128)(2,1)S(1)}, u32[]{:S(2)}, u32[]{:S(2)}) collective-permute-start(bf16[16,768]{1,0:T(8,128)(2,1)S(1)} %get-tuple-element.32), channel_id=1, source_target_pairs={{0,8},{8,16},{16,24},{24,32},{32,40},{40,48},{48,56},{56,64},{64,7... | collective-permute-start | bytes 73736 | tf_op jit(solution)/shard_map/ppermute | solution.py:32
  19.8 7.3 %collective-permute-start.3 = (bf16[16,768]{1,0:T(8,128)(2,1)S(1)}, bf16[16,768]{1,0:T(8,128)(2,1)S(1)}, u32[]{:S(2)}, u32[]{:S(2)}) collective-permute-start(bf16[16,768]{1,0:T(8,128)(2,1)S(1)} %get-tuple-element.33), channel_id=1, source_target_pairs={{8,0},{16,8},{24,16},{32,24},{40,32},{48,40},{56,48},{64,56},{72,6... | collective-permute-start | bytes 73736 | tf_op jit(solution)/shard_map/ppermute | solution.py:34
  27.0 0.0 collective-permute-done.2
  27.1 1.5 %collective-permute-done.3 = bf16[16,768]{1,0:T(8,128)(2,1)S(1)} collective-permute-done((bf16[16,768]{1,0:T(8,128)(2,1)S(1)}, bf16[16,768]{1,0:T(8,128)(2,1)S(1)}, u32[]{:S(2)}, u32[]{:S(2)}) %collective-permute-start.3) | collective-permute-done | bytes 24608 | tf_op jit(solution)/shard_map/ppermute | solution.py:34
  28.5 0.0 copy-done.6
  28.6 1.0 multiply_reduce_fusion
  29.5 0.1 multiply_convert_fusion.1
  29.7 1.9 %collective-permute-start.4 = (bf16[64,768]{1,0:T(8,128)(2,1)S(1)}, bf16[64,768]{1,0:T(8,128)(2,1)S(1)}, u32[]{:S(2)}, u32[]{:S(2)}) collective-permute-start(bf16[64,768]{1,0:T(8,128)(2,1)S(1)} %get-tuple-element.30), channel_id=1, source_target_pairs={{0,8},{8,16},{16,24},{24,32},{32,40},{40,48},{48,56},{56,64},{64,7... | collective-permute-start | bytes 294920 | tf_op jit(solution)/shard_map/ppermute | solution.py:32
  31.6 7.3 %collective-permute-start.5 = (bf16[64,768]{1,0:T(8,128)(2,1)S(1)}, bf16[64,768]{1,0:T(8,128)(2,1)S(1)}, u32[]{:S(2)}, u32[]{:S(2)}) collective-permute-start(bf16[64,768]{1,0:T(8,128)(2,1)S(1)} %get-tuple-element.31), channel_id=1, source_target_pairs={{8,0},{16,8},{24,16},{32,24},{40,32},{48,40},{56,48},{64,56},{72,6... | collective-permute-start | bytes 294920 | tf_op jit(solution)/shard_map/ppermute | solution.py:34
  38.9 0.4 collective-permute-done.4
  39.3 1.8 %collective-permute-done.5 = bf16[64,768]{1,0:T(8,128)(2,1)S(1)} collective-permute-done((bf16[64,768]{1,0:T(8,128)(2,1)S(1)}, bf16[64,768]{1,0:T(8,128)(2,1)S(1)}, u32[]{:S(2)}, u32[]{:S(2)}) %collective-permute-start.5) | collective-permute-done | bytes 98336 | tf_op jit(solution)/shard_map/ppermute | solution.py:34
  41.1 1.8 %convert_reduce_fusion = (f32[16,768]{1,0:T(8,128)S(1)}, bf16[256,768]{1,0:T(8,128)(2,1)}) fusion(f32[256,768]{1,0:T(8,128)S(1)} %get-tuple-element.41, bf16[3,768,768]{2,1,0:T(8,128)(2,1)S(1)} %copy-done.6, bf16[256,768]{1,0:T(8,128)(2,1)S(1)} %multiply_convert_fusion.1, bf16[64,768]{1,0:T(8,128)(2,1)S(1)} %collective-permute-done.5, ...), kind=kOutput, calls=%fused_computation.76 | convolution fusion | flops 309645312 | bytes 3018752 | tf_op jit(solution)/shard_map/dot_general | solution.py:65
  42.9 0.0 copy-start.4
  42.9 0.0 copy-start.3
  42.9 0.9 stack.2
  43.8 7.4 %all-to-all-start = ((bf16[32,16,768]{2,1,0:T(8,128)(2,1)}), bf16[32,16,768]{2,1,0:T(8,128)(2,1)S(1)}, u32[]{:S(2)}, u32[]{:S(2)}) async-start(bf16[32,16,768]{2,1,0:T(8,128)(2,1)} %stack.2), calls=%async_computation | async-start | bytes 1572864 | tf_op jit(solution)/shard_map/all_to_all | solution.py:16
  51.3 0.0 copy-done.4
  51.3 0.1 fusion.29
  51.4 22.2 %all-to-all-done = bf16[32,16,768]{2,1,0:T(8,128)(2,1)S(1)} async-done(((bf16[32,16,768]{2,1,0:T(8,128)(2,1)}), bf16[32,16,768]{2,1,0:T(8,128)(2,1)S(1)}, u32[]{:S(2)}, u32[]{:S(2)}) %all-to-all-start) | async-done | bytes 786464 | tf_op jit(solution)/shard_map/all_to_all | solution.py:16
  73.6 0.0 copy-done.3
  73.6 0.4 fusion.28
  74.0 0.5 multiply_convert_fusion
  74.5 1.9 %collective-permute-start.6 = (bf16[1,512,128]{2,1,0:T(8,128)(2,1)S(1)}, bf16[1,512,128]{2,1,0:T(8,128)(2,1)S(1)}, u32[]{:S(2)}, u32[]{:S(2)}) collective-permute-start(bf16[1,512,128]{2,1,0:T(8,128)(2,1)S(1)} %get-tuple-element.28), channel_id=1, source_target_pairs={{0,8},{8,16},{16,24},{24,32},{32,40},{40,48},{48,56},{56,64},{64,7... | collective-permute-start | bytes 393224 | tf_op jit(solution)/shard_map/ppermute | solution.py:32
  76.4 7.4 %collective-permute-start.7 = (bf16[1,512,128]{2,1,0:T(8,128)(2,1)S(1)}, bf16[1,512,128]{2,1,0:T(8,128)(2,1)S(1)}, u32[]{:S(2)}, u32[]{:S(2)}) collective-permute-start(bf16[1,512,128]{2,1,0:T(8,128)(2,1)S(1)} %get-tuple-element.29), channel_id=1, source_target_pairs={{8,0},{16,8},{24,16},{32,24},{40,32},{48,40},{56,48},{64,56},{72,6... | collective-permute-start | bytes 393224 | tf_op jit(solution)/shard_map/ppermute | solution.py:34
  83.9 0.5 collective-permute-done.6
  84.4 1.8 %collective-permute-done.7 = bf16[1,512,128]{2,1,0:T(8,128)(2,1)S(1)} collective-permute-done((bf16[1,512,128]{2,1,0:T(8,128)(2,1)S(1)}, bf16[1,512,128]{2,1,0:T(8,128)(2,1)S(1)}, u32[]{:S(2)}, u32[]{:S(2)}) %collective-permute-start.7) | collective-permute-done | bytes 131104 | tf_op jit(solution)/shard_map/ppermute | solution.py:34
  86.2 1.4 %fusion.15 = bf16[18,514,128]{2,1,0:T(8,128)(2,1)S(1)} fusion(bf16[1,512,128]{2,1,0:T(8,128)(2,1)S(1)} %collective-permute-done.7, bf16[16,512,128]{2,1,0:T(8,128)(2,1)S(1)} %multiply_convert_fusion, bf16[1,512,128]{2,1,0:T(8,128)(2,1)S(1)} %collective-permute-done.6), kind=kLoop, calls=%fused_computation.26 | loop fusion | flops 14211072 | bytes 4727808 | tf_op jit(solution)/shard_map/concatenate | solution.py:30
  87.6 0.0 copy-start.2
  87.6 3.8 %fusion.133 = (bf16[16,512,128]{2,1,0:T(8,128)(2,1)S(1)}, bf16[16,512,128]{2,1,0:T(8,128)(2,1)S(1)}, bf16[16,512,128]{2,1,0:T(8,128)(2,1)S(1)}, bf16[16,512,128]...) fusion(bf16[18,514,128]{2,1,0:T(8,128)(2,1)S(1)} %fusion.15), kind=kLoop, calls=%fused_computation.199 | loop fusion | bytes 25165824 | tf_op jit(solution)/shard_map/slice | solution.py:75
  91.4 0.0 copy-done.2
  91.4 0.7 fusion.107
  92.1 0.7 fusion.98
  92.8 0.4 pad_maximum_fusion
  93.2 0.7 convolution_add_fusion.6
  93.9 0.7 convolution_add_fusion.5
  94.6 0.7 convolution_add_fusion.4
  95.3 0.7 convolution_add_fusion.3
  95.9 0.7 convolution_add_fusion.2
  96.6 0.7 convolution_add_fusion.1
  97.3 0.0 copy-start.1
  97.4 3.3 %fusion.10 = bf16[8192,128]{1,0:T(8,128)(2,1)} fusion(f32[8192,128]{1,0:T(8,128)S(1)} %fusion.98, f32[8192,128]{1,0:T(8,128)S(1)} %convolution_add_fusion.1, bf16[8192,128]{1,0:T(8,128)(2,1)S(1)} %bitcast.82, bf16[8192,128]{1,0:T(8,128)(2,1)S(1)} %bitcast.73, bf16[3,3,128,128]{3,2,1,0:T(8,128)(2,1)S(1)} %copy-done.2), kind=kOutput, calls=%fused_computation.20 | convolution fusion | flops 282066944 | bytes 14712832 | tf_op jit(solution)/shard_map/dot_general | solution.py:78
  100.7 0.0 copy-done.1
  (9 shorter events, 0.1 us)
Async XLA Ops:
  0.6 2.3 %copy-start = (bf16[512,768]{1,0:T(8,128)(2,1)S(1)}, bf16[512,768]{1,0:T(8,128)(2,1)}, u32[]{:S(2)}) copy-start(bf16[512,768]{1,0:T(8,128)(2,1)} %param.9) | copy-start | bytes 2359300
  2.6 11.1 %copy-start.5 = (f32[3,5,768]{2,0,1:T(4,128)S(1)}, f32[3,5,768]{2,0,1:T(4,128)}, u32[]{:S(2)}) copy-start(f32[3,5,768]{2,0,1:T(4,128)} %param.11) | copy-start | bytes 138244
  3.8 10.1 %collective-permute-start = (bf16[4,768]{1,0:T(4,128)(2,1)S(1)}, bf16[4,768]{1,0:T(4,128)(2,1)S(1)}, u32[]{:S(2)}, u32[]{:S(2)}) collective-permute-start(bf16[4,768]{1,0:T(4,128)(2,1)S(1)} %get-tuple-element.34), channel_id=1, source_target_pairs={{0,8},{8,16},{16,24},{24,32},{32,40},{40,48},{48,56},{56,64},{64,7... | collective-permute-start | bytes 18440 | tf_op jit(solution)/shard_map/ppermute | solution.py:32
  5.7 9.4 %collective-permute-start.1 = (bf16[4,768]{1,0:T(4,128)(2,1)S(1)}, bf16[4,768]{1,0:T(4,128)(2,1)S(1)}, u32[]{:S(2)}, u32[]{:S(2)}) collective-permute-start(bf16[4,768]{1,0:T(4,128)(2,1)S(1)} %get-tuple-element.35), channel_id=1, source_target_pairs={{8,0},{16,8},{24,16},{32,24},{40,32},{48,40},{56,48},{64,56},{72,6... | collective-permute-start | bytes 18440 | tf_op jit(solution)/shard_map/ppermute | solution.py:34
  15.1 13.4 %copy-start.6 = (bf16[3,768,768]{2,1,0:T(8,128)(2,1)S(1)}, bf16[3,768,768]{2,1,0:T(8,128)(2,1)}, u32[]{:S(2)}) copy-start(bf16[3,768,768]{2,1,0:T(8,128)(2,1)} %param.12) | copy-start | bytes 10616836
  17.9 9.2 %collective-permute-start.2 = (bf16[16,768]{1,0:T(8,128)(2,1)S(1)}, bf16[16,768]{1,0:T(8,128)(2,1)S(1)}, u32[]{:S(2)}, u32[]{:S(2)}) collective-permute-start(bf16[16,768]{1,0:T(8,128)(2,1)S(1)} %get-tuple-element.32), channel_id=1, source_target_pairs={{0,8},{8,16},{16,24},{24,32},{32,40},{40,48},{48,56},{56,64},{64,7... | collective-permute-start | bytes 73736 | tf_op jit(solution)/shard_map/ppermute | solution.py:32
  19.8 8.8 %collective-permute-start.3 = (bf16[16,768]{1,0:T(8,128)(2,1)S(1)}, bf16[16,768]{1,0:T(8,128)(2,1)S(1)}, u32[]{:S(2)}, u32[]{:S(2)}) collective-permute-start(bf16[16,768]{1,0:T(8,128)(2,1)S(1)} %get-tuple-element.33), channel_id=1, source_target_pairs={{8,0},{16,8},{24,16},{32,24},{40,32},{48,40},{56,48},{64,56},{72,6... | collective-permute-start | bytes 73736 | tf_op jit(solution)/shard_map/ppermute | solution.py:34
  29.7 9.6 %collective-permute-start.4 = (bf16[64,768]{1,0:T(8,128)(2,1)S(1)}, bf16[64,768]{1,0:T(8,128)(2,1)S(1)}, u32[]{:S(2)}, u32[]{:S(2)}) collective-permute-start(bf16[64,768]{1,0:T(8,128)(2,1)S(1)} %get-tuple-element.30), channel_id=1, source_target_pairs={{0,8},{8,16},{16,24},{24,32},{32,40},{40,48},{48,56},{56,64},{64,7... | collective-permute-start | bytes 294920 | tf_op jit(solution)/shard_map/ppermute | solution.py:32
  31.6 9.5 %collective-permute-start.5 = (bf16[64,768]{1,0:T(8,128)(2,1)S(1)}, bf16[64,768]{1,0:T(8,128)(2,1)S(1)}, u32[]{:S(2)}, u32[]{:S(2)}) collective-permute-start(bf16[64,768]{1,0:T(8,128)(2,1)S(1)} %get-tuple-element.31), channel_id=1, source_target_pairs={{8,0},{16,8},{24,16},{32,24},{40,32},{48,40},{56,48},{64,56},{72,6... | collective-permute-start | bytes 294920 | tf_op jit(solution)/shard_map/ppermute | solution.py:34
  42.9 8.4 %copy-start.4 = (bf16[768,128]{1,0:T(8,128)(2,1)S(1)}, bf16[768,128]{1,0:T(8,128)(2,1)}, u32[]{:S(2)}) copy-start(bf16[768,128]{1,0:T(8,128)(2,1)} %param.13) | copy-start | bytes 589828
  42.9 30.7 %copy-start.3 = (bf16[768,128]{1,0:T(8,128)(2,1)S(1)}, bf16[768,128]{1,0:T(8,128)(2,1)}, u32[]{:S(2)}) copy-start(bf16[768,128]{1,0:T(8,128)(2,1)} %param.14) | copy-start | bytes 589828
  43.8 29.8 %all-to-all-start = ((bf16[32,16,768]{2,1,0:T(8,128)(2,1)}), bf16[32,16,768]{2,1,0:T(8,128)(2,1)S(1)}, u32[]{:S(2)}, u32[]{:S(2)}) async-start(bf16[32,16,768]{2,1,0:T(8,128)(2,1)} %stack.2), calls=%async_computation | async-start | bytes 1572864 | tf_op jit(solution)/shard_map/all_to_all | solution.py:16
  74.5 9.9 %collective-permute-start.6 = (bf16[1,512,128]{2,1,0:T(8,128)(2,1)S(1)}, bf16[1,512,128]{2,1,0:T(8,128)(2,1)S(1)}, u32[]{:S(2)}, u32[]{:S(2)}) collective-permute-start(bf16[1,512,128]{2,1,0:T(8,128)(2,1)S(1)} %get-tuple-element.28), channel_id=1, source_target_pairs={{0,8},{8,16},{16,24},{24,32},{32,40},{40,48},{48,56},{56,64},{64,7... | collective-permute-start | bytes 393224 | tf_op jit(solution)/shard_map/ppermute | solution.py:32
  76.4 9.8 %collective-permute-start.7 = (bf16[1,512,128]{2,1,0:T(8,128)(2,1)S(1)}, bf16[1,512,128]{2,1,0:T(8,128)(2,1)S(1)}, u32[]{:S(2)}, u32[]{:S(2)}) collective-permute-start(bf16[1,512,128]{2,1,0:T(8,128)(2,1)S(1)} %get-tuple-element.29), channel_id=1, source_target_pairs={{8,0},{16,8},{24,16},{32,24},{40,32},{48,40},{56,48},{64,56},{72,6... | collective-permute-start | bytes 393224 | tf_op jit(solution)/shard_map/ppermute | solution.py:34
  87.6 3.8 %copy-start.2 = (bf16[3,3,128,128]{3,2,1,0:T(8,128)(2,1)S(1)}, bf16[3,3,128,128]{3,2,1,0:T(8,128)(2,1)}, u32[]{:S(2)}) copy-start(bf16[3,3,128,128]{3,2,1,0:T(8,128)(2,1)} %param.15) | copy-start | bytes 884740
  97.3 3.3 %copy-start.1 = (bf16[512,768]{1,0:T(8,128)(2,1)S(1)}, bf16[512,768]{1,0:T(8,128)(2,1)}, u32[]{:S(2)}) copy-start(bf16[512,768]{1,0:T(8,128)(2,1)} %param.9) | copy-start | bytes 2359300
